TPU v7x, 512 devices: a whole 4x4x16 slice. The times are simulated.
512 devices in a mesh: dom: 8 (over z_lo), orb: 64 (over x, y, z_hi, core).
Axes of the slice: x: 4, y: 4, z: 16 (z_hi: 2, z_lo: 8; z = z_hi * 8 + z_lo), core: 2. Of those that a mesh axis runs over, the one named last changes fastest.
Arguments:
- orbitals: float32 [8, 320, 12, 16, 128], P('dom', 'orb'), may hold values from -6 to 6
- potential: float32 [8, 12, 16, 128], P('dom'), may hold values from -3 to 0
- projectors: float32 [16, 8, 512], replicated, may hold values from -0.25 to 0.25
- projector_energy: float32 [8], replicated, may hold values from 20 to 160
- atom_first: int32 [16], replicated, may hold values from 0 to 23
- atom_second: int32 [16], replicated, may hold values from 0 to 31
- atom_third: int32 [16], replicated, may hold values from 0 to 255
- rotation: bfloat16 [320, 320], P('orb'), may hold values from -0.3125 to 0.3125
Outputs:
- rotated: bfloat16 [8, 320, 12, 16, 128], P('dom', 'orb')
All inputs are finite; a program needn't handle non-finite values.
Results may differ from a plain program's by a relative error of at most 0.0049.
Values may be sent and summed in bfloat16 or wider, within the bound.
A program may use at most 64 MiB of HBM per device.

v0:
```python
import jax
import jax.numpy as jnp
import numpy as np
from jax import lax
from jax.sharding import PartitionSpec as P

SIDE = 8
SUP = 512
stencil_weights = (
    -5369.0 / 1800.0,
    12.0 / 7.0,
    -15.0 / 56.0,
    10.0 / 189.0,
    -1.0 / 112.0,
    2.0 / 1925.0,
    -1.0 / 16632.0,
)
inverse_spacing = 4.0
filter_center = 120.0
filter_width = 110.0
stencil_reach = 6


def partner_2(block, axis, bit):
    count = lax.axis_size(axis)
    route = []
    for low in range(count):
        high = low | 1 << bit
        if high != low and high < count:
            route += [(low, high), (high, low)]
    return lax.ppermute(block, axis, route)


def outgoing(values, direction, width):
    extent = values.shape[direction]
    if 2 * width < extent:
        return jnp.concatenate(
            (
                lax.slice_in_dim(values, 0, width, axis=direction),
                lax.slice_in_dim(values, extent - width, extent, axis=direction),
            ),
            axis=direction,
        )
    return values


def assemble(values, partner, direction, width):
    extent = values.shape[direction]
    if 2 * width < extent:
        lower_rim = lax.slice_in_dim(partner, width, 2 * width, axis=direction)
        upper_rim = lax.slice_in_dim(partner, 0, width, axis=direction)
        return jnp.concatenate((lower_rim, values, upper_rim), axis=direction)
    cyclic = jnp.concatenate((values, partner), axis=direction)
    chosen = np.arange(-width, extent + width) % (2 * extent)
    return jnp.take(cyclic, jnp.asarray(chosen, dtype=jnp.int32), axis=direction)


def face_padded(values, direction, bit_number):
    sent = outgoing(values, direction, stencil_reach)
    partner = partner_2(sent.astype(jnp.bfloat16), "dom", bit_number).astype(sent.dtype)
    return assemble(values, partner, direction, stencil_reach)


def stencil_sum(center, along):
    lead = center.ndim - 3
    summed = 3.0 * stencil_weights[0] * center
    for index in range(3):
        direction = lead + index
        extent = center.shape[direction]
        padded = along[index]
        for offset in range(1, 7):
            upward = lax.slice_in_dim(
                padded, stencil_reach + offset, stencil_reach + offset + extent, axis=direction
            )
            downward = lax.slice_in_dim(
                padded, stencil_reach - offset, stencil_reach - offset + extent, axis=direction
            )
            summed = summed + stencil_weights[offset] * (upward + downward)
    return summed


def support_map(atom_coords, starts, extents, periods):
    offsets = jnp.arange(SIDE, dtype=jnp.int32) - SIDE // 2
    clipped_list = []
    inside_list = []
    for index in range(3):
        local = (atom_coords[index][:, None] + offsets[None, :] - starts[index]) % periods[index]
        inside_list.append(local < extents[index])
        clipped_list.append(jnp.minimum(local, extents[index] - 1))
    inside = (
        inside_list[0][:, :, None, None]
        & inside_list[1][:, None, :, None]
        & inside_list[2][:, None, None, :]
    )
    flattened = (
        clipped_list[0][:, :, None, None] * extents[1] + clipped_list[1][:, None, :, None]
    ) * extents[2] + clipped_list[2][:, None, None, :]
    atom_count = atom_coords[0].shape[0]
    return (
        flattened.reshape(atom_count * SUP),
        inside.reshape(atom_count, SUP).astype(jnp.float32),
    )


def coefficients(values, support, inside, projectors):
    orbital_count = values.shape[0]
    atom_count = projectors.shape[0]
    flattened = values.reshape(orbital_count, -1)
    picked = (
        jnp.take(flattened, support, axis=1).reshape(orbital_count, atom_count, SUP) * inside[None]
    )
    partial_coeffs = jnp.einsum("aps,kas->kap", projectors, picked, precision=lax.Precision.HIGHEST)
    return lax.psum(partial_coeffs, "dom")


def spread_into(coeffs, shape, support, inside, projectors, projector_energy):
    orbital_count = shape[0]
    atom_count = projectors.shape[0]
    scaled = coeffs * projector_energy[None, None, :]
    spread = (
        jnp.einsum("aps,kap->kas", projectors, scaled, precision=lax.Precision.HIGHEST)
        * inside[None]
    )
    total_cells = shape[1] * shape[2] * shape[3]
    projected_part = (
        jnp.zeros((orbital_count, total_cells), jnp.float32)
        .at[:, support]
        .add(spread.reshape(orbital_count, atom_count * SUP))
    )
    return projected_part.reshape(shape)


def own_hamiltonian(center, along, local_field, support, inside, projectors, projector_energy):
    kinetic = -0.5 * inverse_spacing * inverse_spacing
    coeffs = coefficients(center, support, inside, projectors)
    projected_part = spread_into(
        coeffs, center.shape, support, inside, projectors, projector_energy
    )
    return kinetic * stencil_sum(center, along) + local_field[None] * center + projected_part


def body(
    orbitals, potential, projectors, projector_energy, atom_first, atom_second, atom_third, rotation
):
    domain_count = lax.axis_size("dom")
    domain_bits = domain_count.bit_length() - 1
    split = [index < domain_bits for index in range(3)]
    start_values = orbitals[0]
    local_field = potential[0]
    extents = start_values.shape[1:]
    periods = (
        extents[0] * min(domain_count, 2),
        extents[1] * min(max(domain_count // 2, 1), 2),
        extents[2] * max(domain_count // 4, 1),
    )
    domain_index = lax.axis_index("dom")
    anchors = (
        domain_index % 2 * extents[0],
        domain_index // 2 % 2 * extents[1],
        domain_index // 4 * extents[2],
    )
    atom_coords = (atom_first, atom_second, atom_third)
    support, inside = support_map(atom_coords, anchors, extents, periods)
    along = [face_padded(start_values, index + 1, index) for index in range(3)]
    first_apply = own_hamiltonian(
        start_values, along, local_field, support, inside, projectors, projector_energy
    )
    first_term = (first_apply - filter_center * start_values) / filter_width
    along = [face_padded(first_term, index + 1, index) for index in range(3)]
    second_apply = own_hamiltonian(
        first_term, along, local_field, support, inside, projectors, projector_energy
    )
    second_term = 2.0 * (second_apply - filter_center * first_term) / filter_width - start_values
    per_device = start_values.shape[0]
    filtered = second_term.astype(jnp.bfloat16).reshape(per_device, -1)
    by_cells = lax.all_to_all(filtered, "orb", split_axis=1, concat_axis=0, tiled=True)
    whole_rotation = lax.all_gather(rotation, "orb", axis=0, tiled=True)
    rotated = lax.dot_general(
        whole_rotation, by_cells, (((0,), (0,)), ((), ())), preferred_element_type=jnp.float32
    ).astype(jnp.bfloat16)
    result = lax.all_to_all(rotated, "orb", split_axis=0, concat_axis=1, tiled=True)
    return result.reshape((1,) + start_values.shape)


def solution(mesh):
    return jax.shard_map(
        body,
        mesh=mesh,
        in_specs=(
            P("dom", "orb", None, None, None),
            P("dom", None, None, None),
            P(),
            P(),
            P(),
            P(),
            P(),
            P("orb", None),
        ),
        out_specs=P("dom", "orb", None, None, None),
        check_vma=False,
    )
```

profile of v0, /device:TPU:1, one launch (start us, length us, event | category | flops | bytes accessed | tf_op | source)
XLA Modules:
  0.0 617.4 jit_solution(15906306912854920774)
XLA Ops:
  0.0 1.1 copy.95
  1.1 4.4 collective-permute-start
  5.8 8.8 %collective-permute-start.2 = (bf16[5,12,16,12]{3,2,0,1:T(8,128)(2,1)S(1)}, bf16[5,12,16,12]{3,2,0,1:T(8,128)(2,1)S(1)}, u32[]{:S(2)}, u32[]{:S(2)}) collective-permute-start(bf16[5,12,16,12]{3,2,0,1:T(8,128)(2,1)S(1)} %pad_maximum_fusion.11), channel_id=1, source_target_pairs={{0,256},{256,0},{64,320},{320,64},{128,384},{384,128},{192,448},{4... | collective-permute-start | bytes 69128 | tf_op jit(solution)/shard_map/ppermute | solution.py:31
  14.7 0.8 pad_maximum_fusion.10
  15.5 4.9 collective-permute-start.1
  20.4 0.8 minimum_multiply_fusion
  21.2 0.8 fusion.162
  22.0 7.9 %copy.69 = f32[1,5,12,16,128]{1,4,3,2,0:T(8,128)} copy(f32[1,5,12,16,128]{4,3,2,1,0:T(8,128)} %param.14) | data formatting | bytes 983040 | tf_op args[0]
  31.2 32.3 %gather_fusion.1 = f32[8192,5]{1,0:T(8,128)} fusion(f32[5,24576]{0,1:T(8,128)} %bitcast.59, s32[8192]{0:T(1024)S(1)} %fusion.157), kind=kCustom, calls=%fused_computation.1.clone | custom fusion | bytes 360448 | tf_op jit(solution)/shard_map/jit(_take)/gather | solution.py:110
  63.5 7.5 %broadcast_select_fusion.1 = f32[8192,5]{1,0:T(8,128)} fusion(f32[8192,5]{1,0:T(8,128)} %gather_fusion.1, pred[8192]{0:T(1024)(128)(4,1)S(1)} %compare_and_fusion), kind=kLoop, calls=%fused_computation.11 | loop fusion | flops 40960 | bytes 335872 | tf_op jit(solution)/shard_map/jit(_take)/select_n | solution.py:110
  70.9 2.9 copy.71
  73.8 0.6 convolution_bitcast_fusion.1
  74.5 42.7 %psum.14 = f32[5,16,8]{2,0,1:T(8,128)S(1)} all-reduce(f32[5,16,8]{2,0,1:T(8,128)S(1)} %convolution_bitcast_fusion.1), channel_id=1, replica_groups=mesh['dom'=8,'orb'=64] {'dom'}, use_global_device_ids=true, to_apply=%region_0.3 | all-reduce | flops 640 | bytes 5120 | tf_op jit(solution)/shard_map/psum | solution.py:113
  117.2 0.7 broadcast_multiply_fusion.1
  118.3 2.6 copy.73
  120.9 54.2 %scatter_custom_fusion = f32[5,24576]{0,1:T(8,128)} fusion(s32[8192]{0:T(1024)S(1)} %bitcast.74, f32[8192,5]{1,0:T(8,128)} %copy.73, f32[]{:T(128)} %constant.127.clone.1), kind=kCustom, calls=%fused_computation.8 | custom fusion | flops 40960 | bytes 492032 | tf_op jit(solution)/shard_map/scatter-add | solution.py:128
  175.1 8.3 %copy.74 = f32[5,12,16,128]{3,2,0,1:T(8,128)} copy(f32[5,12,16,128]{0,3,2,1:T(8,128)} %bitcast.56) | data formatting | bytes 983040 | tf_op jit(solution)/shard_map/reshape | solution.py:130
  183.4 1.0 fusion.177
  184.5 0.7 fusion.175
  185.3 0.6 gather_fusion
  186.0 6.8 %fusion.168 = (bf16[5,12,16,128]{3,2,0,1:T(8,128)(2,1)S(1)}, f32[5,12,16,128]{3,2,0,1:T(8,128)S(1)}) fusion(f32[5,12,16,128]{3,2,0,1:T(8,128)S(1)} %bitcast.64, f32[5,12,16,128]{3,2,0,1:T(8,128)} %copy.74, f32[12,16,128]{2,1,0:T(8,128)} %bitcast.73, f32[5,12,16,6]{3,2,0,1:T(8,128)} %get-tuple-element.22, f32[5,12,16,6]{3,2,0,1:T(8,128)} %get-tuple-element.21, ...), kind=kLoop, calls=%fused_computation.309 | loop fusion | flops 10690560 | bytes 8131584 | tf_op jit(solution)/shard_map/convert_element_type | solution.py:60
  193.0 2.1 collective-permute-start.3
  195.2 6.6 %copy.85 = f32[5,12,16,128]{0,3,2,1:T(8,128)} copy(f32[5,12,16,128]{3,2,0,1:T(8,128)S(1)} %broadcast_multiply_fusion) | data formatting | bytes 983040 | tf_op jit(solution)/shard_map/reshape | solution.py:108
  201.8 32.3 %gather_fusion.3 = f32[8192,5]{1,0:T(8,128)} fusion(f32[5,24576]{0,1:T(8,128)} %bitcast.60, s32[8192]{0:T(1024)S(1)} %fusion.157), kind=kCustom, calls=%fused_computation.3.clone | custom fusion | bytes 360448 | tf_op jit(solution)/shard_map/jit(_take)/gather | solution.py:110
  234.1 7.5 %broadcast_select_fusion = f32[8192,5]{1,0:T(8,128)} fusion(f32[8192,5]{1,0:T(8,128)} %gather_fusion.3, pred[8192]{0:T(1024)(128)(4,1)S(1)} %compare_and_fusion), kind=kLoop, calls=%fused_computation.10 | loop fusion | flops 40960 | bytes 335872 | tf_op jit(solution)/shard_map/jit(_take)/select_n | solution.py:110
  241.5 2.8 copy.78
  244.4 0.6 convolution_bitcast_fusion
  245.0 43.8 %psum.15 = f32[5,16,8]{2,0,1:T(8,128)S(1)} all-reduce(f32[5,16,8]{2,0,1:T(8,128)S(1)} %convolution_bitcast_fusion), channel_id=1, replica_groups=mesh['dom'=8,'orb'=64] {'dom'}, use_global_device_ids=true, to_apply=%region_2.5 | all-reduce | flops 640 | bytes 5120 | tf_op jit(solution)/shard_map/psum | solution.py:113
  288.8 0.4 convolution_multiply_fusion
  289.2 0.8 pad_maximum_fusion.13
  290.0 1.9 collective-permute-start.5
  292.0 2.6 copy.79
  294.7 54.2 %scatter_custom_fusion.1 = f32[5,24576]{0,1:T(8,128)} fusion(s32[8192]{0:T(1024)} %bitcast.75, f32[8192,5]{1,0:T(8,128)} %copy.79, f32[]{:T(128)} %constant.127.clone.1), kind=kCustom, calls=%fused_computation.6 | custom fusion | flops 40960 | bytes 492032 | tf_op jit(solution)/shard_map/scatter-add | solution.py:128
  348.9 7.6 %copy.81 = f32[5,12,16,128]{3,2,0,1:T(8,128)S(1)} copy(f32[5,12,16,128]{0,3,2,1:T(8,128)} %bitcast.55) | data formatting | bytes 983040 | tf_op jit(solution)/shard_map/reshape | solution.py:130
  356.5 2.4 collective-permute-start.4
  358.9 1.1 fusion.173
  360.0 5.0 collective-permute-done.4
  365.0 0.8 fusion.171
  365.8 1.0 convert_element_type.54
  366.8 1.0 copy.75
  367.9 1.9 gather_fusion.2
  369.8 7.5 %subtract_convert_fusion = bf16[5,12,16,128]{3,2,0,1:T(8,128)(2,1)S(1)} fusion(f32[5,12,16,128]{3,2,0,1:T(8,128)S(1)} %get-tuple-element.8, f32[5,12,16,128]{3,2,0,1:T(8,128)S(1)} %copy.81, f32[5,12,16,128]{3,2,0,1:T(8,128)S(1)} %broadcast_multiply_fusion, f32[5,12,16,6]{3,2,0,1:T(8,128)} %get-tuple-element.14, f32[5,12,16,6]{3,2,0,1:T(8,128)} %get-tuple-element.13, ...), kind=kLoop, calls=%fused_computation.265 | loop fusion | flops 10813440 | bytes 8623104 | tf_op jit(solution)/shard_map/convert_element_type | solution.py:175
  377.5 0.9 copy.83
  378.4 34.7 %all-to-all-start = ((bf16[5,64,384]{2,0,1:T(8,128)(2,1)}), bf16[5,64,384]{2,0,1:T(8,128)(2,1)S(1)}, u32[]{:S(2)}, u32[]{:S(2)}) async-start(bf16[5,64,384]{2,0,1:T(8,128)(2,1)} %copy.83), calls=%async_computation | async-start | bytes 786432 | tf_op jit(solution)/shard_map/all_to_all | solution.py:176
  413.1 172.7 %all-gather = bf16[64,5,320]{2,1,0:T(8,128)(2,1)S(1)} all-gather(bf16[1,5,320]{2,1,0:T(8,128)(2,1)} %bitcast.76), channel_id=1, replica_groups=mesh['dom'=8,'orb'=64] {'orb'}, dimensions={0}, use_global_device_ids=true | all-gather | bytes 208000 | tf_op jit(solution)/shard_map/all_gather | solution.py:177
  586.1 0.4 fusion.4
  586.5 30.0 %all_to_all.35 = bf16[64,5,384]{2,1,0:T(8,128)(2,1)S(1)} all-to-all(bf16[64,5,384]{2,1,0:T(8,128)(2,1)S(1)} %all_to_all.30), channel_id=1, replica_groups=mesh['dom'=8,'orb'=64] {'orb'}, dimensions={0} | all-to-all | bytes 491520 | tf_op jit(solution)/shard_map/all_to_all | solution.py:181
  616.6 0.8 reshape.300
  (55 shorter events, 3.0 us)
Async XLA Ops:
  0.0 73.8 %copy-start = (f32[16,8,512]{2,1,0:T(8,128)S(1)}, f32[16,8,512]{2,1,0:T(8,128)}, u32[]{:S(2)}) copy-start(f32[16,8,512]{2,1,0:T(8,128)} %param.16) | copy-start | bytes 786436
  1.1 184.1 %collective-permute-start = (bf16[5,12,16,128]{3,2,0,1:T(8,128)(2,1)S(1)}, bf16[5,12,16,128]{3,2,0,1:T(8,128)(2,1)S(1)}, u32[]{:S(2)}, u32[]{:S(2)}) collective-permute-start(bf16[5,12,16,128]{3,2,0,1:T(8,128)(2,1)S(1)} %bitcast.65), channel_id=1, source_target_pairs={{0,64},{64,0},{128,192},{192,128},{256,320},{320,256},{384,448},{4... | collective-permute-start | bytes 737288 | tf_op jit(solution)/shard_map/ppermute | solution.py:31
  5.8 177.7 %collective-permute-start.2 = (bf16[5,12,16,12]{3,2,0,1:T(8,128)(2,1)S(1)}, bf16[5,12,16,12]{3,2,0,1:T(8,128)(2,1)S(1)}, u32[]{:S(2)}, u32[]{:S(2)}) collective-permute-start(bf16[5,12,16,12]{3,2,0,1:T(8,128)(2,1)S(1)} %pad_maximum_fusion.11), channel_id=1, source_target_pairs={{0,256},{256,0},{64,320},{320,64},{128,384},{384,128},{192,448},{4... | collective-permute-start | bytes 69128 | tf_op jit(solution)/shard_map/ppermute | solution.py:31
  15.5 169.0 %collective-permute-start.1 = (bf16[5,12,12,128]{3,2,0,1:T(8,128)(2,1)}, bf16[5,12,12,128]{3,2,0,1:T(8,128)(2,1)S(1)}, u32[]{:S(2)}, u32[]{:S(2)}) collective-permute-start(bf16[5,12,12,128]{3,2,0,1:T(8,128)(2,1)} %pad_maximum_fusion.10), channel_id=1, source_target_pairs={{0,128},{128,0},{64,192},{192,64},{256,384},{384,256},{320,448},{4... | collective-permute-start | bytes 552968 | tf_op jit(solution)/shard_map/ppermute | solution.py:31
  31.0 89.9 %copy-start.4 = (s32[8192,1]{0,1:T(1,128)}, s32[8192,1]{0,1:T(1,128)S(1)}, u32[]{:S(2)}) copy-start(s32[8192,1]{0,1:T(1,128)S(1)} %compare_select_fusion) | copy-start | bytes 98308
  70.9 46.2 %copy-start.2 = (f32[1,12,16,128]{3,2,1,0:T(8,128)S(1)}, f32[1,12,16,128]{3,2,1,0:T(8,128)}, u32[]{:S(2)}) copy-start(f32[1,12,16,128]{3,2,1,0:T(8,128)} %param.15) | copy-start | bytes 294916
  70.9 46.9 %copy-start.6 = (f32[8]{0:T(128)S(1)}, f32[8]{0:T(128)}, u32[]{:S(2)}) copy-start(f32[8]{0:T(128)} %param.17) | copy-start | bytes 100
  70.9 47.3 %copy-start.7 = (s32[24]{0:T(128)S(1)}, s32[24]{0:T(128)}, u32[]{:S(2)}) copy-start(s32[24]{0:T(128)} %constant.175) | copy-start | bytes 292
  70.9 47.3 %copy-start.1 = (f32[1,5,12,16,128]{4,3,2,1,0:T(8,128)S(1)}, f32[1,5,12,16,128]{4,3,2,1,0:T(8,128)}, u32[]{:S(2)}) copy-start(f32[1,5,12,16,128]{4,3,2,1,0:T(8,128)} %param.14) | copy-start | bytes 1474564
  118.2 67.1 %copy-start.5 = (s32[1024]{0:T(1024)}, s32[1024]{0:T(1024)S(1)}, u32[]{:S(2)}) copy-start(s32[1024]{0:T(1024)S(1)} %pad_clamp_fusion) | copy-start | bytes 12292
  193.0 172.8 %collective-permute-start.3 = (bf16[5,12,16,128]{3,2,0,1:T(8,128)(2,1)S(1)}, bf16[5,12,16,128]{3,2,0,1:T(8,128)(2,1)}, u32[]{:S(2)}, u32[]{:S(2)}) collective-permute-start(bf16[5,12,16,128]{3,2,0,1:T(8,128)(2,1)S(1)} %get-tuple-element.6), channel_id=1, source_target_pairs={{0,64},{64,0},{128,192},{192,128},{256,320},{320,256},{384,448},{4... | collective-permute-start | bytes 737288 | tf_op jit(solution)/shard_map/ppermute | solution.py:31
  290.0 68.9 %collective-permute-start.5 = (bf16[5,12,16,12]{3,2,0,1:T(8,128)(2,1)}, bf16[5,12,16,12]{3,2,0,1:T(8,128)(2,1)S(1)}, u32[]{:S(2)}, u32[]{:S(2)}) collective-permute-start(bf16[5,12,16,12]{3,2,0,1:T(8,128)(2,1)} %pad_maximum_fusion.13), channel_id=1, source_target_pairs={{0,256},{256,0},{64,320},{320,64},{128,384},{384,128},{192,448},{4... | collective-permute-start | bytes 69128 | tf_op jit(solution)/shard_map/ppermute | solution.py:31
  356.5 8.5 %collective-permute-start.4 = (bf16[5,12,12,128]{3,2,0,1:T(8,128)(2,1)S(1)}, bf16[5,12,12,128]{3,2,0,1:T(8,128)(2,1)S(1)}, u32[]{:S(2)}, u32[]{:S(2)}) collective-permute-start(bf16[5,12,12,128]{3,2,0,1:T(8,128)(2,1)S(1)} %pad_maximum_fusion.12), channel_id=1, source_target_pairs={{0,128},{128,0},{64,192},{192,64},{256,384},{384,256},{320,448},{4... | collective-permute-start | bytes 552968 | tf_op jit(solution)/shard_map/ppermute | solution.py:31
  360.0 9.8 %copy-start.3 = (f32[12,16,128]{2,1,0:T(8,128)S(1)}, f32[12,16,128]{2,1,0:T(8,128)}, u32[]{:S(2)}) copy-start(f32[12,16,128]{2,1,0:T(8,128)} %broadcast_multiply_fusion.1) | copy-start | bytes 294916
  378.4 207.5 %all-to-all-start = ((bf16[5,64,384]{2,0,1:T(8,128)(2,1)}), bf16[5,64,384]{2,0,1:T(8,128)(2,1)S(1)}, u32[]{:S(2)}, u32[]{:S(2)}) async-start(bf16[5,64,384]{2,0,1:T(8,128)(2,1)} %copy.83), calls=%async_computation | async-start | bytes 786432 | tf_op jit(solution)/shard_map/all_to_all | solution.py:176
where the time goes:
time: 619 us; the launch traced here: 617 us
  blocking collectives  289 us (47%)
  other arithmetic  143 us (23%)
  local copies, waits for them, and re-layouts  118 us (19%)
  starting transfers between devices  59.1 us (10%)
    all_gather x1, blocking collectives, body(): whole_rotation = lax.all_gather(rotation, 'orb', axis=0, tiled=True)  173 us
    scatter-add x2, other arithmetic, spread_into(): projected_part = jnp.zeros((orbital_count, total_cells), jnp.float32).at[...  108 us
    psum x2, blocking collectives, coefficients(): return lax.psum(partial_coeffs, 'dom')  86.5 us
    gather x2, local copies, waits for them, and re-layouts, coefficients(): jnp.take(flattened, support, axis=1).reshape(orbital_count, atom_count, SUP)  64.6 us
    all_to_all x1, starting transfers between devices, body(): lax.all_to_all(filtered, 'orb', split_axis=1, concat_axis=0, tiled=True)  34.7 us
    all_to_all x1, blocking collectives, body(): lax.all_to_all(rotated, 'orb', split_axis=0, concat_axis=1, tiled=True)  30 us
    ppermute x6, starting transfers between devices, partner_2(): return lax.ppermute(block, axis, route)  24.5 us
    reshape x2, local copies, waits for them, and re-layouts, spread_into(): return projected_part.reshape(shape)  15.9 us
  transfers between devices with their start and end apart: 7, of which 1 were waited for; matrix products, arithmetic and copies ran while one was open for 39% of the time, Pallas kernels for 0%

commit v1 on v0

--- a/solution.py
+++ b/solution.py
@@ -19,6 +19,11 @@
 filter_center = 120.0
 filter_width = 110.0
 stencil_reach = 6
+
+
+def gather_and_add(x, name):
+    shards = lax.all_gather(x, name)
+    return jnp.sum(shards, axis=0)
 
 
 def partner_2(block, axis, bit):
@@ -110,7 +115,7 @@
         jnp.take(flattened, support, axis=1).reshape(orbital_count, atom_count, SUP) * inside[None]
     )
     partial_coeffs = jnp.einsum("aps,kas->kap", projectors, picked, precision=lax.Precision.HIGHEST)
-    return lax.psum(partial_coeffs, "dom")
+    return gather_and_add(partial_coeffs, "dom")
 
 
 def spread_into(coeffs, shape, support, inside, projectors, projector_energy):

time: 619 us -> 607 us (0.981); the launches traced: 617 us -> 598 us
  blocking collectives: 289 us -> 274 us
    psum x2 -> x0, blocking collectives: 86.5 us -> none  [coefficients(): return lax.psum(partial_coeffs, 'dom')]
    all_gather x0 -> x2, blocking collectives: none -> 80.5 us  [gather_and_add(): shards = lax.all_gather(x, name)]
    all_to_all x1, blocking collectives: 30 us -> 23.8 us  [body(): lax.all_to_all(rotated, 'orb', split_axis=0, concat_axis=1, tiled=True)]
  transfers between devices with their start and end apart: 7 -> 7, of which waited for: 1 -> 1; matrix products, arithmetic and copies ran while one was open for 39% -> 40% of each run, Pallas kernels for 0% -> 0%
where the time goes in v1:
time: 607 us; the launch traced here: 598 us
  blocking collectives  274 us (45%)
  other arithmetic  142 us (23%)
  local copies, waits for them, and re-layouts  119 us (20%)
  starting transfers between devices  53.9 us (9%)
    all_gather x1, blocking collectives, body(): whole_rotation = lax.all_gather(rotation, 'orb', axis=0, tiled=True)  170 us
    scatter-add x2, other arithmetic, spread_into(): projected_part = jnp.zeros((orbital_count, total_cells), jnp.float32).at[...  108 us
    all_gather x2, blocking collectives, gather_and_add(): shards = lax.all_gather(x, name)  80.5 us
    gather x2, local copies, waits for them, and re-layouts, coefficients(): jnp.take(flattened, support, axis=1).reshape(orbital_count, atom_count, SUP)  64.9 us
    all_to_all x1, starting transfers between devices, body(): lax.all_to_all(filtered, 'orb', split_axis=1, concat_axis=0, tiled=True)  29.4 us
    ppermute x6, starting transfers between devices, partner_2(): return lax.ppermute(block, axis, route)  24.5 us
    all_to_all x1, blocking collectives, body(): lax.all_to_all(rotated, 'orb', split_axis=0, concat_axis=1, tiled=True)  23.8 us
    reshape x2, local copies, waits for them, and re-layouts, spread_into(): return projected_part.reshape(shape)  15.9 us
  transfers between devices with their start and end apart: 7, of which 1 were waited for; matrix products, arithmetic and copies ran while one was open for 40% of the time, Pallas kernels for 0%

profile of v1, /device:TPU:1, one launch (start us, length us, event | category | flops | bytes accessed | tf_op | source)
XLA Modules:
  0.0 598.0 jit_solution(10635500518361943930)
XLA Ops:
  0.0 1.1 copy.107
  1.1 4.4 collective-permute-start
  5.8 8.8 %collective-permute-start.2 = (bf16[5,12,16,12]{3,2,0,1:T(8,128)(2,1)S(1)}, bf16[5,12,16,12]{3,2,0,1:T(8,128)(2,1)S(1)}, u32[]{:S(2)}, u32[]{:S(2)}) collective-permute-start(bf16[5,12,16,12]{3,2,0,1:T(8,128)(2,1)S(1)} %pad_maximum_fusion.11), channel_id=1, source_target_pairs={{0,256},{256,0},{64,320},{320,64},{128,384},{384,128},{192,448},{4... | collective-permute-start | bytes 69128 | tf_op jit(solution)/shard_map/ppermute | solution.py:36
  14.7 0.8 pad_maximum_fusion.10
  15.5 4.9 collective-permute-start.1
  20.4 7.9 %copy.77 = f32[1,5,12,16,128]{1,4,3,2,0:T(8,128)} copy(f32[1,5,12,16,128]{4,3,2,1,0:T(8,128)} %param.14) | data formatting | bytes 983040 | tf_op args[0]
  28.9 0.3 add.461
  29.7 32.5 %gather_fusion.1 = f32[8192,5]{1,0:T(8,128)} fusion(f32[5,24576]{0,1:T(8,128)} %bitcast.63, s32[8192]{0:T(1024)S(1)} %fusion.153), kind=kCustom, calls=%fused_computation.1.clone | custom fusion | bytes 360448 | tf_op jit(solution)/shard_map/jit(_take)/gather | solution.py:115
  62.1 7.5 %broadcast_select_fusion.1 = f32[8192,5]{1,0:T(8,128)} fusion(f32[8192,5]{1,0:T(8,128)} %gather_fusion.1, pred[8192]{0:T(1024)(128)(4,1)S(1)} %compare_and_fusion), kind=kLoop, calls=%fused_computation.11 | loop fusion | flops 40960 | bytes 335872 | tf_op jit(solution)/shard_map/jit(_take)/select_n | solution.py:115
  69.6 2.9 copy.79
  72.7 0.6 convolution_bitcast_fusion.1
  73.4 40.1 %all-gather = f32[40,16,8]{1,2,0:T(8,128)S(1)} all-gather(f32[5,16,8]{1,2,0:T(8,128)S(1)} %copy.80), channel_id=2, replica_groups=mesh['dom'=8,'orb'=64] {'dom'}, dimensions={0}, use_global_device_ids=true | all-gather | bytes 23040 | tf_op jit(solution)/shard_map/all_gather | solution.py:25
  113.7 0.4 convolution_multiply_fusion.1
  114.1 0.6 broadcast_multiply_fusion.1
  114.8 2.6 copy.83
  117.4 54.2 %scatter_custom_fusion = f32[5,24576]{0,1:T(8,128)} fusion(s32[8192]{0:T(1024)S(1)} %bitcast.80, f32[8192,5]{1,0:T(8,128)} %copy.83, f32[]{:T(128)} %constant.128.clone.1), kind=kCustom, calls=%fused_computation.8 | custom fusion | flops 40960 | bytes 492032 | tf_op jit(solution)/shard_map/scatter-add | solution.py:133
  171.7 8.3 %copy.84 = f32[5,12,16,128]{3,2,0,1:T(8,128)} copy(f32[5,12,16,128]{0,3,2,1:T(8,128)} %bitcast.60) | data formatting | bytes 983040 | tf_op jit(solution)/shard_map/reshape | solution.py:135
  180.0 1.0 fusion.173
  181.0 0.7 fusion.171
  181.9 0.6 gather_fusion
  182.5 7.0 %fusion.164 = (bf16[5,12,16,128]{3,2,0,1:T(8,128)(2,1)S(1)}, f32[5,12,16,128]{3,2,0,1:T(8,128)S(1)}) fusion(f32[5,12,16,128]{3,2,0,1:T(8,128)S(1)} %bitcast.68, f32[5,12,16,128]{3,2,0,1:T(8,128)} %copy.84, f32[12,16,128]{2,1,0:T(8,128)} %bitcast.79, f32[5,12,16,6]{3,2,0,1:T(8,128)} %get-tuple-element.22, f32[5,12,16,6]{3,2,0,1:T(8,128)} %get-tuple-element.21, ...), kind=kLoop, calls=%fused_computation.307 | loop fusion | flops 10690560 | bytes 8131584 | tf_op jit(solution)/shard_map/convert_element_type | solution.py:65
  189.7 2.1 collective-permute-start.3
  191.9 6.6 %copy.97 = f32[5,12,16,128]{0,3,2,1:T(8,128)} copy(f32[5,12,16,128]{3,2,0,1:T(8,128)S(1)} %broadcast_multiply_fusion) | data formatting | bytes 983040 | tf_op jit(solution)/shard_map/reshape | solution.py:113
  198.5 32.5 %gather_fusion.3 = f32[8192,5]{1,0:T(8,128)} fusion(f32[5,24576]{0,1:T(8,128)} %bitcast.64, s32[8192]{0:T(1024)S(1)} %fusion.153), kind=kCustom, calls=%fused_computation.3.clone | custom fusion | bytes 360448 | tf_op jit(solution)/shard_map/jit(_take)/gather | solution.py:115
  231.0 7.5 %broadcast_select_fusion = f32[8192,5]{1,0:T(8,128)} fusion(f32[8192,5]{1,0:T(8,128)} %gather_fusion.3, pred[8192]{0:T(1024)(128)(4,1)S(1)} %compare_and_fusion), kind=kLoop, calls=%fused_computation.10 | loop fusion | flops 40960 | bytes 335872 | tf_op jit(solution)/shard_map/jit(_take)/select_n | solution.py:115
  238.4 2.8 copy.88
  241.3 0.6 convolution_bitcast_fusion
  242.0 40.4 %all-gather.1 = f32[40,16,8]{1,2,0:T(8,128)S(1)} all-gather(f32[5,16,8]{1,2,0:T(8,128)S(1)} %copy.89), channel_id=3, replica_groups=mesh['dom'=8,'orb'=64] {'dom'}, dimensions={0}, use_global_device_ids=true | all-gather | bytes 23040 | tf_op jit(solution)/shard_map/all_gather | solution.py:25
  282.6 0.4 convolution_multiply_fusion
  283.0 0.8 pad_maximum_fusion.13
  283.8 1.9 collective-permute-start.5
  285.8 2.6 copy.91
  288.5 54.2 %scatter_custom_fusion.1 = f32[5,24576]{0,1:T(8,128)} fusion(s32[8192]{0:T(1024)} %bitcast.81, f32[8192,5]{1,0:T(8,128)} %copy.91, f32[]{:T(128)} %constant.128.clone.1), kind=kCustom, calls=%fused_computation.6 | custom fusion | flops 40960 | bytes 492032 | tf_op jit(solution)/shard_map/scatter-add | solution.py:133
  342.7 7.6 %copy.93 = f32[5,12,16,128]{3,2,0,1:T(8,128)S(1)} copy(f32[5,12,16,128]{0,3,2,1:T(8,128)} %bitcast.59) | data formatting | bytes 983040 | tf_op jit(solution)/shard_map/reshape | solution.py:135
  350.3 2.4 collective-permute-start.4
  352.7 1.1 fusion.169
  353.8 6.0 %collective-permute-done.4 = bf16[5,12,12,128]{3,2,0,1:T(8,128)(2,1)S(1)} collective-permute-done((bf16[5,12,12,128]{3,2,0,1:T(8,128)(2,1)S(1)}, bf16[5,12,12,128]{3,2,0,1:T(8,128)(2,1)S(1)}, u32[]{:S(2)}, u32[]{:S(2)}) %collective-permute-start.4) | collective-permute-done | bytes 184352 | tf_op jit(solution)/shard_map/ppermute | solution.py:36
  359.8 0.8 fusion.167
  360.6 1.0 convert_element_type.54
  361.6 1.1 copy.85
  362.7 1.9 gather_fusion.2
  364.6 7.5 %subtract_convert_fusion = bf16[5,12,16,128]{3,2,0,1:T(8,128)(2,1)S(1)} fusion(f32[5,12,16,128]{3,2,0,1:T(8,128)S(1)} %get-tuple-element.8, f32[5,12,16,128]{3,2,0,1:T(8,128)S(1)} %copy.93, f32[5,12,16,128]{3,2,0,1:T(8,128)S(1)} %broadcast_multiply_fusion, f32[5,12,16,6]{3,2,0,1:T(8,128)} %get-tuple-element.14, f32[5,12,16,6]{3,2,0,1:T(8,128)} %get-tuple-element.13, ...), kind=kLoop, calls=%fused_computation.265 | loop fusion | flops 10813440 | bytes 8623104 | tf_op jit(solution)/shard_map/convert_element_type | solution.py:180
  372.3 0.9 copy.95
  373.2 29.4 %all-to-all-start = ((bf16[5,64,384]{2,0,1:T(8,128)(2,1)}), bf16[5,64,384]{2,0,1:T(8,128)(2,1)S(1)}, u32[]{:S(2)}, u32[]{:S(2)}) async-start(bf16[5,64,384]{2,0,1:T(8,128)(2,1)} %copy.95), calls=%async_computation | async-start | bytes 786432 | tf_op jit(solution)/shard_map/all_to_all | solution.py:181
  402.6 170.0 %all-gather.2 = bf16[64,5,320]{2,1,0:T(8,128)(2,1)S(1)} all-gather(bf16[1,5,320]{2,1,0:T(8,128)(2,1)} %bitcast.82), channel_id=1, replica_groups=mesh['dom'=8,'orb'=64] {'orb'}, dimensions={0}, use_global_device_ids=true | all-gather | bytes 208000 | tf_op jit(solution)/shard_map/all_gather | solution.py:182
  572.9 0.4 fusion.4
  573.4 23.8 %all_to_all.35 = bf16[64,5,384]{2,1,0:T(8,128)(2,1)S(1)} all-to-all(bf16[64,5,384]{2,1,0:T(8,128)(2,1)S(1)} %all_to_all.30), channel_id=1, replica_groups=mesh['dom'=8,'orb'=64] {'orb'}, dimensions={0} | all-to-all | bytes 491520 | tf_op jit(solution)/shard_map/all_to_all | solution.py:186
  597.2 0.8 reshape.300
  (69 shorter events, 3.1 us)
Async XLA Ops:
  0.0 72.7 %copy-start = (f32[16,8,512]{2,1,0:T(8,128)S(1)}, f32[16,8,512]{2,1,0:T(8,128)}, u32[]{:S(2)}) copy-start(f32[16,8,512]{2,1,0:T(8,128)} %param.16) | copy-start | bytes 786436
  1.1 180.6 %collective-permute-start = (bf16[5,12,16,128]{3,2,0,1:T(8,128)(2,1)S(1)}, bf16[5,12,16,128]{3,2,0,1:T(8,128)(2,1)S(1)}, u32[]{:S(2)}, u32[]{:S(2)}) collective-permute-start(bf16[5,12,16,128]{3,2,0,1:T(8,128)(2,1)S(1)} %bitcast.69), channel_id=1, source_target_pairs={{0,64},{64,0},{128,192},{192,128},{256,320},{320,256},{384,448},{4... | collective-permute-start | bytes 737288 | tf_op jit(solution)/shard_map/ppermute | solution.py:36
  5.8 174.2 %collective-permute-start.2 = (bf16[5,12,16,12]{3,2,0,1:T(8,128)(2,1)S(1)}, bf16[5,12,16,12]{3,2,0,1:T(8,128)(2,1)S(1)}, u32[]{:S(2)}, u32[]{:S(2)}) collective-permute-start(bf16[5,12,16,12]{3,2,0,1:T(8,128)(2,1)S(1)} %pad_maximum_fusion.11), channel_id=1, source_target_pairs={{0,256},{256,0},{64,320},{320,64},{128,384},{384,128},{192,448},{4... | collective-permute-start | bytes 69128 | tf_op jit(solution)/shard_map/ppermute | solution.py:36
  15.5 165.6 %collective-permute-start.1 = (bf16[5,12,12,128]{3,2,0,1:T(8,128)(2,1)}, bf16[5,12,12,128]{3,2,0,1:T(8,128)(2,1)S(1)}, u32[]{:S(2)}, u32[]{:S(2)}) collective-permute-start(bf16[5,12,12,128]{3,2,0,1:T(8,128)(2,1)} %pad_maximum_fusion.10), channel_id=1, source_target_pairs={{0,128},{128,0},{64,192},{192,64},{256,384},{384,256},{320,448},{4... | collective-permute-start | bytes 552968 | tf_op jit(solution)/shard_map/ppermute | solution.py:36
  20.4 7.9 %copy-start.6 = (s32[16]{0:T(128)S(1)}, s32[16]{0:T(128)}, u32[]{:S(2)}) copy-start(s32[16]{0:T(128)} %param.18) | copy-start | bytes 196
  20.4 7.9 %copy-start.7 = (s32[16]{0:T(128)S(1)}, s32[16]{0:T(128)}, u32[]{:S(2)}) copy-start(s32[16]{0:T(128)} %param.20) | copy-start | bytes 196
  20.4 7.9 %copy-start.8 = (s32[16]{0:T(128)S(1)}, s32[16]{0:T(128)}, u32[]{:S(2)}) copy-start(s32[16]{0:T(128)} %param.19) | copy-start | bytes 196
  29.7 87.8 %copy-start.4 = (s32[8192,1]{0,1:T(1,128)}, s32[8192,1]{0,1:T(1,128)S(1)}, u32[]{:S(2)}) copy-start(s32[8192,1]{0,1:T(1,128)S(1)} %compare_select_fusion) | copy-start | bytes 98308
  69.6 43.9 %copy-start.9 = (f32[8]{0:T(128)S(1)}, f32[8]{0:T(128)}, u32[]{:S(2)}) copy-start(f32[8]{0:T(128)} %param.17) | copy-start | bytes 100
  69.6 44.5 %copy-start.2 = (f32[1,12,16,128]{3,2,1,0:T(8,128)S(1)}, f32[1,12,16,128]{3,2,1,0:T(8,128)}, u32[]{:S(2)}) copy-start(f32[1,12,16,128]{3,2,1,0:T(8,128)} %param.15) | copy-start | bytes 294916
  69.6 45.1 %copy-start.10 = (s32[24]{0:T(128)S(1)}, s32[24]{0:T(128)}, u32[]{:S(2)}) copy-start(s32[24]{0:T(128)} %constant.176) | copy-start | bytes 292
  69.6 45.1 %copy-start.1 = (f32[1,5,12,16,128]{4,3,2,1,0:T(8,128)S(1)}, f32[1,5,12,16,128]{4,3,2,1,0:T(8,128)}, u32[]{:S(2)}) copy-start(f32[1,5,12,16,128]{4,3,2,1,0:T(8,128)} %param.14) | copy-start | bytes 1474564
  114.8 67.1 %copy-start.5 = (s32[1024]{0:T(1024)}, s32[1024]{0:T(1024)S(1)}, u32[]{:S(2)}) copy-start(s32[1024]{0:T(1024)S(1)} %pad_clamp_fusion) | copy-start | bytes 12292
  189.7 170.8 %collective-permute-start.3 = (bf16[5,12,16,128]{3,2,0,1:T(8,128)(2,1)S(1)}, bf16[5,12,16,128]{3,2,0,1:T(8,128)(2,1)}, u32[]{:S(2)}, u32[]{:S(2)}) collective-permute-start(bf16[5,12,16,128]{3,2,0,1:T(8,128)(2,1)S(1)} %get-tuple-element.6), channel_id=1, source_target_pairs={{0,64},{64,0},{128,192},{192,128},{256,320},{320,256},{384,448},{4... | collective-permute-start | bytes 737288 | tf_op jit(solution)/shard_map/ppermute | solution.py:36
  283.8 68.9 %collective-permute-start.5 = (bf16[5,12,16,12]{3,2,0,1:T(8,128)(2,1)}, bf16[5,12,16,12]{3,2,0,1:T(8,128)(2,1)S(1)}, u32[]{:S(2)}, u32[]{:S(2)}) collective-permute-start(bf16[5,12,16,12]{3,2,0,1:T(8,128)(2,1)} %pad_maximum_fusion.13), channel_id=1, source_target_pairs={{0,256},{256,0},{64,320},{320,64},{128,384},{384,128},{192,448},{4... | collective-permute-start | bytes 69128 | tf_op jit(solution)/shard_map/ppermute | solution.py:36
  350.3 9.5 %collective-permute-start.4 = (bf16[5,12,12,128]{3,2,0,1:T(8,128)(2,1)S(1)}, bf16[5,12,12,128]{3,2,0,1:T(8,128)(2,1)S(1)}, u32[]{:S(2)}, u32[]{:S(2)}) collective-permute-start(bf16[5,12,12,128]{3,2,0,1:T(8,128)(2,1)S(1)} %pad_maximum_fusion.12), channel_id=1, source_target_pairs={{0,128},{128,0},{64,192},{192,64},{256,384},{384,256},{320,448},{4... | collective-permute-start | bytes 552968 | tf_op jit(solution)/shard_map/ppermute | solution.py:36
  353.7 10.9 %copy-start.3 = (f32[12,16,128]{2,1,0:T(8,128)S(1)}, f32[12,16,128]{2,1,0:T(8,128)}, u32[]{:S(2)}) copy-start(f32[12,16,128]{2,1,0:T(8,128)} %broadcast_multiply_fusion.1) | copy-start | bytes 294916
  373.2 199.6 %all-to-all-start = ((bf16[5,64,384]{2,0,1:T(8,128)(2,1)}), bf16[5,64,384]{2,0,1:T(8,128)(2,1)S(1)}, u32[]{:S(2)}, u32[]{:S(2)}) async-start(bf16[5,64,384]{2,0,1:T(8,128)(2,1)} %copy.95), calls=%async_computation | async-start | bytes 786432 | tf_op jit(solution)/shard_map/all_to_all | solution.py:181
